TPU v7x, 256 devices: a whole 4x4x8 slice. The times are simulated.
256 devices in a mesh: feat: 8 (over z), dom: 32 (over x, y, core).
Axes of the slice: x: 4, y: 4, z: 8, core: 2. Of those that a mesh axis runs over, the one named last changes fastest.
Arguments:
- features: bfloat16 [128, 32768], P('feat', 'dom'), may hold values from -6 to 6
- self_weight: bfloat16 [128, 512], P('feat'), may hold values from -0.5 to 0.5
- neighbor_weight: bfloat16 [128, 512], P('feat'), may hold values from -0.5 to 0.5
- unit_bias: float32 [512], P('feat'), may hold values from -3 to 3
- send_blocks: int32 [32, 32, 4], P('dom'), may hold values from 0 to 7
- send_counts: int32 [32, 32], P('dom'), may hold values from 0 to 4, as said below
- tile_target: int32 [32, 256], P('dom'), may hold values from 0 to 7
- tile_source: int32 [32, 256], P('dom'), may hold values from 0 to 135, as said below
- tile_count: int32 [32], P('dom'), may hold values from 64 to 256, as said below
- tile_weights: bfloat16 [32, 256, 128, 128], P('dom'), may hold values from 0 to 1, as said below
- out_grad: bfloat16 [512, 32768], P('feat', 'dom'), may hold values from -0.119628906 to 0.119628906
Outputs:
- hidden: bfloat16 [512, 32768], P('feat', 'dom')
- self_gradient: float32 [128, 512], P('feat')
- neighbor_gradient: float32 [128, 512], P('feat')
- bias_gradient: float32 [512], P('feat')
Inputs may be any that keep to these rules, and one draw needn't show every extreme that they name: `send_counts`: the diagonal is 0; each partition d fills all 4 slots toward partitions d - 1 and d + 1 (counted round). `tile_count`: at least one partition has all 256 tiles live. `tile_source`: tile 0 of partition d reads slot 8 + ((d + 1) mod 32) * 4, tile 1 reads slot 8 + ((d - 1) mod 32) * 4. `tile_weights`: entries may be 0.
All inputs are finite; a program needn't handle non-finite values.
Results may differ from a plain program's by a relative error of at most 0.005.
Values may be sent and summed in bfloat16 or wider, within the bound.
A program may use at most 64 MiB of HBM per device.

v0:
```python
import jax
import jax.numpy as jnp
from jax import lax
from jax.sharding import PartitionSpec as P

BLK = 128
BMAX = 4


def activate(values):
    return jax.nn.gelu(values, approximate=True)


def body(
    features,
    self_weight,
    neighbor_weight,
    unit_bias,
    send_blocks,
    send_counts,
    tile_target,
    tile_source,
    tile_count,
    tile_weights,
    out_grad,
):
    row_count = features.shape[1]
    unit_width = out_grad.shape[0]
    own_blocks = row_count // BLK
    neighbor_term = jnp.einsum(
        "fh,fr->hr", neighbor_weight, features, preferred_element_type=jnp.float32
    )
    self_term = jnp.einsum("fh,fr->hr", self_weight, features, preferred_element_type=jnp.float32)
    stacked = lax.psum_scatter(
        jnp.concatenate([neighbor_term, self_term], axis=1), "feat", scatter_dimension=0, tiled=True
    )
    projected = stacked[:, :row_count].astype(jnp.bfloat16)
    self_part = stacked[:, row_count:]
    slot_index = jnp.arange(BMAX, dtype=jnp.int32)
    chosen = send_blocks[0].reshape(-1)
    live_slots = (slot_index[None, :] < send_counts[0][:, None]).reshape(-1)
    own_table = projected.reshape(unit_width, own_blocks, BLK)
    outgoing = jnp.take(own_table, chosen, axis=1) * live_slots.astype(jnp.bfloat16)[None, :, None]
    incoming = lax.all_to_all(
        outgoing.reshape(unit_width, -1), "dom", split_axis=1, concat_axis=1, tiled=True
    )
    slot_table = jnp.concatenate([projected, incoming], axis=1).reshape(unit_width, -1, BLK)
    slot_number = slot_table.shape[1]
    weights = tile_weights[0]
    tile_total = weights.shape[0]
    live_tiles = (jnp.arange(tile_total, dtype=jnp.int32) < tile_count[0]).astype(jnp.float32)
    sources = tile_source[0]
    targets = tile_target[0]
    picked = jnp.take(slot_table, sources, axis=1)
    products = (
        jnp.einsum("htc,trc->thr", picked, weights, preferred_element_type=jnp.float32)
        * live_tiles[:, None, None]
    )
    block_sums = jax.ops.segment_sum(products, targets, num_segments=own_blocks)
    aggregate = jnp.transpose(block_sums, (1, 0, 2)).reshape(unit_width, row_count)
    unit_ones = jnp.ones((weights.shape[2],), jnp.bfloat16)
    row_sums = (
        jnp.einsum("trc,c->tr", weights, unit_ones, preferred_element_type=jnp.float32)
        * live_tiles[:, None]
    )
    degree = 1.0 + jax.ops.segment_sum(row_sums, targets, num_segments=own_blocks).reshape(
        row_count
    )
    summed_input = self_part + aggregate / degree[None, :] + unit_bias[:, None]
    hidden, pullback = jax.vjp(activate, summed_input)
    summed_grad = pullback(out_grad.astype(jnp.float32))[0]
    scaled = (summed_grad / degree[None, :]).astype(jnp.bfloat16)
    target_rows = jnp.take(scaled.reshape(unit_width, own_blocks, BLK), targets, axis=1)
    pushed = (
        jnp.einsum("htr,trc->thc", target_rows, weights, preferred_element_type=jnp.float32)
        * live_tiles[:, None, None]
    )
    slot_totals = jax.ops.segment_sum(pushed, sources, num_segments=slot_number)
    returned = lax.all_to_all(
        slot_totals[own_blocks:], "dom", split_axis=0, concat_axis=0, tiled=True
    )
    returned = returned * live_slots.astype(jnp.float32)[:, None, None]
    folded = (
        jax.ops.segment_sum(returned, chosen, num_segments=own_blocks) + slot_totals[:own_blocks]
    )
    neighbor_totals = (
        jnp.transpose(folded, (1, 0, 2)).reshape(unit_width, row_count).astype(jnp.bfloat16)
    )
    narrow_total = summed_grad.astype(jnp.bfloat16)
    bias_part = jnp.sum(summed_grad, axis=1)
    full_narrow, full_neighbor = (
        lax.all_gather(narrow_total, "feat", axis=0, tiled=True),
        lax.all_gather(neighbor_totals, "feat", axis=0, tiled=True),
    )
    self_term = jnp.einsum("fr,hr->fh", features, full_narrow, preferred_element_type=jnp.float32)
    neighbor_term = jnp.einsum(
        "fr,hr->fh", features, full_neighbor, preferred_element_type=jnp.float32
    )
    self_gradient, neighbor_gradient, bias_gradient = lax.psum(
        (self_term, neighbor_term, bias_part), "dom"
    )
    return (hidden.astype(jnp.bfloat16), self_gradient, neighbor_gradient, bias_gradient)


def solution(mesh):
    in_specs = (
        P("feat", "dom"),
        P("feat", None),
        P("feat", None),
        P("feat"),
        P("dom", None, None),
        P("dom", None),
        P("dom", None),
        P("dom", None),
        P("dom"),
        P("dom", None, None, None),
        P("feat", "dom"),
    )
    out_specs = (P("feat", "dom"), P("feat", None), P("feat", None), P("feat"))
    return jax.shard_map(body, mesh=mesh, in_specs=in_specs, out_specs=out_specs, check_vma=False)
```

profile of v0, /device:TPU:1, one launch (start us, length us, event | category | flops | bytes accessed | tf_op | source)
XLA Modules:
  0.0 458.1 jit_solution(16673961788908352427)
XLA Ops:
  7.2 0.7 copy-done
  7.9 1.2 fusion.48
  9.1 1.2 fusion.47
  10.3 2.4 pad_maximum_fusion
  12.7 0.7 copy-done.4
  13.5 0.1 copy.43
  13.6 0.1 broadcast_in_dim.51
  13.7 0.1 reshape_squeeze.6
  13.9 0.1 mul.88
  14.1 58.0 %reduce-scatter.2.cloned.1.call-done = f32[64,2048]{1,0:T(8,128)} async-done(((f32[512,2048]{1,0:T(8,128)}), f32[64,2048]{1,0:T(8,128)}) %reduce-scatter.2.cloned.1.call-update) | async-done | bytes 524304 | tf_op jit(solution)/shard_map/reduce_scatter | solution.py:34
  72.1 1.0 copy_bitcast_fusion.3
  73.0 1.0 gather_fusion
  74.0 2.7 copy.46
  76.7 3.1 gather.15
  79.8 0.2 select_multiply_fusion
  80.0 2.5 copy.47
  82.5 7.5 %all-to-all-start = ((bf16[64,32,512]{2,0,1:T(8,128)(2,1)}), bf16[64,32,512]{2,0,1:T(8,128)(2,1)S(1)}, u32[]{:S(2)}, u32[]{:S(2)}) async-start(bf16[64,32,512]{2,0,1:T(8,128)(2,1)} %copy.47), calls=%async_computation.1 | async-start | bytes 4194304 | tf_op jit(solution)/shard_map/all_to_all | solution.py:44
  90.7 5.7 %fusion.2 = f32[1,256,128]{2,0,1:T(1,128)S(1)} fusion(bf16[1,256,128,128]{3,2,1,0:T(8,128)(2,1)} %param.20), kind=kOutput, calls=%fused_computation.9 | convolution fusion | flops 8388608 | bytes 8519680 | tf_op jit(solution)/shard_map/trc,c->tr/dot_general | solution.py:63
  96.4 2.2 scatter_custom_fusion.1
  98.7 19.6 %all-to-all-done = bf16[64,32,512]{2,0,1:T(8,128)(2,1)S(1)} async-done(((bf16[64,32,512]{2,0,1:T(8,128)(2,1)}), bf16[64,32,512]{2,0,1:T(8,128)(2,1)S(1)}, u32[]{:S(2)}, u32[]{:S(2)}) %all-to-all-start) | async-done | bytes 2097184 | tf_op jit(solution)/shard_map/all_to_all | solution.py:44
  118.3 0.2 copy.58
  118.5 0.6 copy_bitcast_fusion
  119.1 3.1 gather_fusion.1
  122.2 13.6 %broadcast_multiply_fusion.1 = f32[256,64,128]{2,1,0:T(8,128)} fusion(f32[256]{0:T(256)S(1)} %get-tuple-element.14, bf16[1,256,128,128]{3,2,1,0:T(8,128)(2,1)} %param.20, bf16[256,64,128]{2,1,0:T(8,128)(2,1)} %gather_fusion.1, pred[256]{0:T(512)(128)(4,1)S(1)} %get-tuple-element.15), kind=kOutput, calls=%fused_computation.19 | convolution fusion | flops 541065216 | bytes 20972800 | tf_op jit(solution)/shard_map/htc,trc->thr/dot_general | solution.py:56
  135.9 26.2 %scatter_fusion = f32[8,64,128]{2,1,0:T(8,128)S(1)} fusion(f32[8,64,128]{2,1,0:T(8,128)S(1)} %broadcast.124, s32[256]{0:T(256)S(1)} %bitcast.115, f32[256,64,128]{2,1,0:T(8,128)} %broadcast_multiply_fusion.1), kind=kCustom, calls=%fused_computation.3 | custom fusion | flops 2097152 | bytes 25166848 | tf_op jit(solution)/shard_map/scatter-add | solution.py:59
  162.1 1.6 fusion.45
  163.7 0.7 fusion.35
  164.4 3.1 gather_fusion.2
  167.4 10.3 %broadcast_multiply_fusion = f32[256,64,128]{2,1,0:T(8,128)} fusion(f32[256]{0:T(256)S(1)} %get-tuple-element.14, bf16[1,256,128,128]{3,2,1,0:T(8,128)(2,1)} %param.20, bf16[256,64,128]{2,1,0:T(8,128)(2,1)} %gather_fusion.2, pred[256]{0:T(512)(128)(4,1)S(1)} %compare_and_fusion), kind=kOutput, calls=%fused_computation.18 | convolution fusion | flops 541065216 | bytes 20972800 | tf_op jit(solution)/shard_map/htr,trc->thc/dot_general | solution.py:75
  177.8 2.6 broadcast_in_dim.58
  180.4 39.3 %scatter_fusion.1 = f32[136,64,128]{2,1,0:T(8,128)} fusion(f32[136,64,128]{2,1,0:T(8,128)} %broadcast_in_dim.58, s32[256]{0:T(256)S(1)} %bitcast.112, f32[256,64,128]{2,1,0:T(8,128)} %broadcast_multiply_fusion), kind=kCustom, calls=%fused_computation.5 | custom fusion | flops 2097152 | bytes 25166848 | tf_op jit(solution)/shard_map/scatter-add | solution.py:78
  219.8 4.7 %slice.26 = f32[128,64,128]{2,1,0:T(8,128)} slice(f32[136,64,128]{2,1,0:T(8,128)} %scatter_fusion.1), slice={[8:136], [0:64], [0:128]} | slice | bytes 8388608 | tf_op jit(solution)/shard_map/slice | solution.py:80
  224.5 5.3 %all-to-all-start.1 = ((f32[128,64,128]{2,1,0:T(8,128)}), f32[128,64,128]{2,1,0:T(8,128)}, u32[]{:S(2)}, u32[]{:S(2)}) async-start(f32[128,64,128]{2,1,0:T(8,128)} %slice.26), calls=%async_computation.2 | async-start | bytes 8388608 | tf_op jit(solution)/shard_map/all_to_all | solution.py:79
  229.9 0.7 all-gather.3.cloned.1.call-update
  230.6 0.1 reshape.247
  230.7 0.1 reshape.196
  230.8 1.0 slice.25
  231.8 50.3 %all-to-all-done.1 = f32[128,64,128]{2,1,0:T(8,128)} async-done(((f32[128,64,128]{2,1,0:T(8,128)}), f32[128,64,128]{2,1,0:T(8,128)}, u32[]{:S(2)}, u32[]{:S(2)}) %all-to-all-start.1) | async-done | bytes 4194336 | tf_op jit(solution)/shard_map/all_to_all | solution.py:79
  282.1 4.5 broadcast_multiply_fusion.2
  286.6 13.5 %scatter_fusion.2 = f32[8,64,128]{2,1,0:T(8,128)S(1)} fusion(f32[8,64,128]{2,1,0:T(8,128)S(1)} %slice.25, s32[128]{0:T(128)S(1)} %reshape.247, f32[128,64,128]{2,1,0:T(8,128)} %broadcast_multiply_fusion.2), kind=kCustom, calls=%fused_computation.6 | custom fusion | flops 1048576 | bytes 12583424 | tf_op jit(solution)/shard_map/scatter-add | solution.py:84
  300.2 0.7 copy_bitcast_fusion.1
  300.9 2.2 convolution_bitcast_fusion.1
  303.2 29.7 %all-gather.5.cloned.1.call-done = bf16[512,1024]{1,0:T(8,128)(2,1)} async-done(((bf16[64,1024]{1,0:T(8,128)(2,1)}), bf16[512,1024]{1,0:T(8,128)(2,1)}) %all-gather.5.cloned.1.call-update) | async-done | bytes 1048592 | tf_op jit(solution)/shard_map/all_gather | solution.py:93
  332.9 2.2 convolution_bitcast_fusion
  335.1 112.6 %all-reduce.3.cloned.1.call-done = (f32[16,512]{1,0:T(8,128)}, f32[16,512]{1,0:T(8,128)}, f32[64]{0:T(128)}) async-done(((f32[16,512]{1,0:T(8,128)}, f32[16,512]{1,0:T(8,128)}, f32[64]{0:T(128)}), (f32[16,512]{1,0:T(8,128)}, f32[16,512]{1,0:T(8,128)}, f32[64]{0:T(128)})) %all-reduce.3.cloned.1.call-update) | async-done | bytes 65808 | tf_op jit(solution)/shard_map/psum | solution.py:99
  447.7 1.4 copy.85
  449.1 1.4 copy.86
  450.4 1.1 copy.87
  (38 shorter events, 0.6 us)
Async XLA Ops:
  7.2 0.8 copy-start
  7.2 64.9 %reduce-scatter.2.cloned.1.call-start = ((), (), s32[]{:S(2)}) async-start(), calls=%async_computation.3 | async-start | bytes 4718592 | tf_op jit(solution)/shard_map/reduce_scatter | solution.py:34
  12.7 0.7 copy-start.4
  12.7 1.1 copy-start.7
  80.0 10.6 %copy-start.3 = (s32[1,256]{1,0:T(1,128)S(1)}, s32[1,256]{1,0:T(1,128)}, u32[]{:S(2)}) copy-start(s32[1,256]{1,0:T(1,128)} %param.18) | copy-start | bytes 3076
  82.5 35.8 %all-to-all-start = ((bf16[64,32,512]{2,0,1:T(8,128)(2,1)}), bf16[64,32,512]{2,0,1:T(8,128)(2,1)S(1)}, u32[]{:S(2)}, u32[]{:S(2)}) async-start(bf16[64,32,512]{2,0,1:T(8,128)(2,1)} %copy.47), calls=%async_computation.1 | async-start | bytes 4194304 | tf_op jit(solution)/shard_map/all_to_all | solution.py:44
  90.7 5.7 %copy-start.5 = (s32[1,256]{1,0:T(1,128)S(1)}, s32[1,256]{1,0:T(1,128)}, u32[]{:S(2)}) copy-start(s32[1,256]{1,0:T(1,128)} %param.17) | copy-start | bytes 3076
  90.7 8.0 %copy-start.1 = (f32[64,2048]{1,0:T(8,128)S(1)}, f32[64,2048]{1,0:T(8,128)}, u32[]{:S(2)}) copy-start(f32[64,2048]{1,0:T(8,128)} %reduce-scatter.2.cloned.1.call-done) | copy-start | bytes 1572868
  135.8 26.3 %copy-start.2 = (bf16[64,1024]{1,0:T(8,128)(2,1)S(1)}, bf16[64,1024]{1,0:T(8,128)(2,1)}, u32[]{:S(2)}) copy-start(bf16[64,1024]{1,0:T(8,128)(2,1)} %param.21) | copy-start | bytes 393220
  135.8 26.3 %copy-start.6 = (f32[64]{0:T(128)S(1)}, f32[64]{0:T(128)}, u32[]{:S(2)}) copy-start(f32[64]{0:T(128)} %param.14) | copy-start | bytes 772
  224.5 57.6 %all-to-all-start.1 = ((f32[128,64,128]{2,1,0:T(8,128)}), f32[128,64,128]{2,1,0:T(8,128)}, u32[]{:S(2)}, u32[]{:S(2)}) async-start(f32[128,64,128]{2,1,0:T(8,128)} %slice.26), calls=%async_computation.2 | async-start | bytes 8388608 | tf_op jit(solution)/shard_map/all_to_all | solution.py:79
  229.8 71.1 %all-gather.3.cloned.1.call-start = ((), (), s32[]{:S(2)}) async-start(), calls=%async_computation.4 | async-start | bytes 1179648 | tf_op jit(solution)/shard_map/all_gather | solution.py:92
  230.6 102.3 %all-gather.5.cloned.1.call-start = ((), (), s32[]{:S(2)}) async-start(), calls=%async_computation.5 | async-start | bytes 1179648 | tf_op jit(solution)/shard_map/all_gather | solution.py:93
  300.9 146.8 %all-reduce.3.cloned.1.call-start = ((), (), s32[]{:S(2)}) async-start(), calls=%async_computation.6 | async-start | bytes 132096 | tf_op jit(solution)/shard_map/psum | solution.py:99
Sparse Core Ops, SparseCore 0:
  12.9 59.1 reduce-scatter.1
  232.4 33.6 all-gather.2
  301.0 31.8 all-gather.4
  336.9 110.7 all-reduce.2
where the time goes:
time: 460 us; the launch traced here: 458 us
  waiting for transfers between devices  271 us (59%)
  other arithmetic  92.1 us (20%)
  matrix products  36.5 us (8%)
  local copies, waits for them, and re-layouts  30.9 us (7%)
  between operations  14.7 us (3%)
  starting transfers between devices  12.9 us (3%)
    psum x1, waiting for transfers between devices, body(): lax.psum((self_term, neighbor_term, bias_part), 'dom')  113 us
    reduce_scatter x1, waiting for transfers between devices, body(): lax.psum_scatter(jnp.concatenate([neighbor_term, self_term], axis=1), 'fe...  58 us
    all_to_all x1, waiting for transfers between devices, body(): lax.all_to_all(slot_totals[own_blocks:], 'dom', split_axis=0, concat_axis...  50.3 us
    scatter-add x1, other arithmetic, body(): slot_totals = jax.ops.segment_sum(pushed, sources, num_segments=slot_number)  39.3 us
    all_gather x1, waiting for transfers between devices, body(): lax.all_gather(neighbor_totals, 'feat', axis=0, tiled=True)  29.7 us
    scatter-add x1, other arithmetic, body(): block_sums = jax.ops.segment_sum(products, targets, num_segments=own_blocks)  26.2 us
    all_to_all x1, waiting for transfers between devices, body(): lax.all_to_all(outgoing.reshape(unit_width, -1), 'dom', split_axis=1, con...  19.6 us
    dot_general x1, matrix products, body(): jnp.einsum('htc,trc->thr', picked, weights, preferred_element_type=jnp.fl...  13.6 us
  transfers between devices with their start and end apart: 6, of which 5 were waited for; matrix products, arithmetic and copies ran while one was open for 7% of the time, Pallas kernels for 0%

commit v1 on v0

--- a/solution.py
+++ b/solution.py
@@ -90,7 +90,10 @@
     bias_part = jnp.sum(summed_grad, axis=1)
     full_narrow, full_neighbor = (
         lax.all_gather(narrow_total, "feat", axis=0, tiled=True),
-        lax.all_gather(neighbor_totals, "feat", axis=0, tiled=True),
+        jnp.concatenate(
+            lax.all_to_all(jnp.stack(lax.axis_size("feat") * [neighbor_totals]), "feat", 0, 0),
+            axis=0,
+        ),
     )
     self_term = jnp.einsum("fr,hr->fh", features, full_narrow, preferred_element_type=jnp.float32)
     neighbor_term = jnp.einsum(

time: 460 us -> 452 us (0.983)
  waiting for transfers between devices: 271 us -> 258 us
    all_gather x1 -> x0, waiting for transfers between devices: 29.7 us -> none  [body(): lax.all_gather(neighbor_totals, 'feat', axis=0, tiled=True)]
    all_to_all x0 -> x1, waiting for transfers between devices: none -> 26.9 us  [body(): lax.all_to_all(jnp.stack(lax.axis_size('feat') * [neighbor_totals]), 'fea...]
    psum x1, waiting for transfers between devices: 113 us -> 103 us  [body(): lax.psum((self_term, neighbor_term, bias_part), 'dom')]
where the time goes in v1:
time: 452 us; the launch traced here: 449 us
  waiting for transfers between devices  258 us (57%)
  other arithmetic  91.9 us (20%)
  matrix products  35.2 us (8%)
  local copies, waits for them, and re-layouts  32 us (7%)
  starting transfers between devices  17.1 us (4%)
  between operations  14.7 us (3%)
    psum x1, waiting for transfers between devices, body(): lax.psum((self_term, neighbor_term, bias_part), 'dom')  103 us
    reduce_scatter x1, waiting for transfers between devices, body(): lax.psum_scatter(jnp.concatenate([neighbor_term, self_term], axis=1), 'fe...  58 us
    all_to_all x1, waiting for transfers between devices, body(): lax.all_to_all(slot_totals[own_blocks:], 'dom', split_axis=0, concat_axis...  51 us
    scatter-add x1, other arithmetic, body(): slot_totals = jax.ops.segment_sum(pushed, sources, num_segments=slot_number)  39.7 us
    all_to_all x1, waiting for transfers between devices, body(): lax.all_to_all(jnp.stack(lax.axis_size('feat') * [neighbor_totals]), 'fea...  26.9 us
    scatter-add x1, other arithmetic, body(): block_sums = jax.ops.segment_sum(products, targets, num_segments=own_blocks)  26.2 us
    all_to_all x1, waiting for transfers between devices, body(): lax.all_to_all(outgoing.reshape(unit_width, -1), 'dom', split_axis=1, con...  19.6 us
    dot_general x1, matrix products, body(): jnp.einsum('htc,trc->thr', picked, weights, preferred_element_type=jnp.fl...  13.6 us
  transfers between devices with their start and end apart: 6, of which 5 were waited for; matrix products, arithmetic and copies ran while one was open for 7% of the time, Pallas kernels for 0%

profile of v1, /device:TPU:1, one launch (start us, length us, event | category | flops | bytes accessed | tf_op | source)
XLA Modules:
  0.0 449.2 jit_solution(14402341093006155556)
XLA Ops:
  7.2 0.7 copy-done
  7.9 1.2 fusion.48
  9.1 1.2 fusion.47
  10.3 2.4 pad_maximum_fusion
  12.7 0.7 copy-done.4
  13.5 0.1 copy.43
  13.6 0.1 broadcast_in_dim.51
  13.7 0.1 reshape_squeeze.6
  13.9 0.1 mul.88
  14.0 58.0 %reduce-scatter.2.cloned.1.call-done = f32[64,2048]{1,0:T(8,128)} async-done(((f32[512,2048]{1,0:T(8,128)}), f32[64,2048]{1,0:T(8,128)}) %reduce-scatter.2.cloned.1.call-update) | async-done | bytes 524304 | tf_op jit(solution)/shard_map/reduce_scatter | solution.py:34
  72.1 1.0 copy_bitcast_fusion.3
  73.0 1.0 gather_fusion
  74.0 2.7 copy.46
  76.7 3.1 gather.15
  79.8 0.2 select_multiply_fusion
  80.0 2.5 copy.47
  82.5 7.5 %all-to-all-start = ((bf16[64,32,512]{2,0,1:T(8,128)(2,1)}), bf16[64,32,512]{2,0,1:T(8,128)(2,1)S(1)}, u32[]{:S(2)}, u32[]{:S(2)}) async-start(bf16[64,32,512]{2,0,1:T(8,128)(2,1)} %copy.47), calls=%async_computation.1 | async-start | bytes 4194304 | tf_op jit(solution)/shard_map/all_to_all | solution.py:44
  90.7 5.7 %fusion.2 = f32[1,256,128]{2,0,1:T(1,128)S(1)} fusion(bf16[1,256,128,128]{3,2,1,0:T(8,128)(2,1)} %param.20), kind=kOutput, calls=%fused_computation.9 | convolution fusion | flops 8388608 | bytes 8519680 | tf_op jit(solution)/shard_map/trc,c->tr/dot_general | solution.py:63
  96.4 2.2 scatter_custom_fusion.1
  98.7 19.6 %all-to-all-done = bf16[64,32,512]{2,0,1:T(8,128)(2,1)S(1)} async-done(((bf16[64,32,512]{2,0,1:T(8,128)(2,1)}), bf16[64,32,512]{2,0,1:T(8,128)(2,1)S(1)}, u32[]{:S(2)}, u32[]{:S(2)}) %all-to-all-start) | async-done | bytes 2097184 | tf_op jit(solution)/shard_map/all_to_all | solution.py:44
  118.3 0.2 copy.58
  118.5 0.6 copy_bitcast_fusion
  119.1 3.1 gather_fusion.1
  122.2 13.6 %broadcast_multiply_fusion.1 = f32[256,64,128]{2,1,0:T(8,128)} fusion(f32[256]{0:T(256)S(1)} %get-tuple-element.14, bf16[1,256,128,128]{3,2,1,0:T(8,128)(2,1)} %param.20, bf16[256,64,128]{2,1,0:T(8,128)(2,1)} %gather_fusion.1, pred[256]{0:T(512)(128)(4,1)S(1)} %get-tuple-element.15), kind=kOutput, calls=%fused_computation.19 | convolution fusion | flops 541065216 | bytes 20972800 | tf_op jit(solution)/shard_map/htc,trc->thr/dot_general | solution.py:56
  135.8 26.2 %scatter_fusion = f32[8,64,128]{2,1,0:T(8,128)S(1)} fusion(f32[8,64,128]{2,1,0:T(8,128)S(1)} %broadcast.125, s32[256]{0:T(256)S(1)} %bitcast.117, f32[256,64,128]{2,1,0:T(8,128)} %broadcast_multiply_fusion.1), kind=kCustom, calls=%fused_computation.3 | custom fusion | flops 2097152 | bytes 25166848 | tf_op jit(solution)/shard_map/scatter-add | solution.py:59
  162.1 1.6 fusion.45
  163.7 0.7 fusion.35
  164.4 3.1 gather_fusion.2
  167.4 10.4 %broadcast_multiply_fusion = f32[256,64,128]{2,1,0:T(8,128)} fusion(f32[256]{0:T(256)S(1)} %get-tuple-element.14, bf16[1,256,128,128]{3,2,1,0:T(8,128)(2,1)} %param.20, bf16[256,64,128]{2,1,0:T(8,128)(2,1)} %gather_fusion.2, pred[256]{0:T(512)(128)(4,1)S(1)} %compare_and_fusion), kind=kOutput, calls=%fused_computation.18 | convolution fusion | flops 541065216 | bytes 20972800 | tf_op jit(solution)/shard_map/htr,trc->thc/dot_general | solution.py:75
  177.8 2.6 broadcast_in_dim.58
  180.4 39.7 %scatter_fusion.1 = f32[136,64,128]{2,1,0:T(8,128)} fusion(f32[136,64,128]{2,1,0:T(8,128)} %broadcast_in_dim.58, s32[256]{0:T(256)S(1)} %bitcast.114, f32[256,64,128]{2,1,0:T(8,128)} %broadcast_multiply_fusion), kind=kCustom, calls=%fused_computation.5 | custom fusion | flops 2097152 | bytes 25166848 | tf_op jit(solution)/shard_map/scatter-add | solution.py:78
  220.2 4.8 %slice.26 = f32[128,64,128]{2,1,0:T(8,128)} slice(f32[136,64,128]{2,1,0:T(8,128)} %scatter_fusion.1), slice={[8:136], [0:64], [0:128]} | slice | bytes 8388608 | tf_op jit(solution)/shard_map/slice | solution.py:80
  224.9 5.4 %all-to-all-start.1 = ((f32[128,64,128]{2,1,0:T(8,128)}), f32[128,64,128]{2,1,0:T(8,128)}, u32[]{:S(2)}, u32[]{:S(2)}) async-start(f32[128,64,128]{2,1,0:T(8,128)} %slice.26), calls=%async_computation.2 | async-start | bytes 8388608 | tf_op jit(solution)/shard_map/all_to_all | solution.py:79
  230.4 0.1 reshape.254
  230.5 0.1 reshape.203
  230.6 1.0 slice.25
  231.6 51.0 %all-to-all-done.1 = f32[128,64,128]{2,1,0:T(8,128)} async-done(((f32[128,64,128]{2,1,0:T(8,128)}), f32[128,64,128]{2,1,0:T(8,128)}, u32[]{:S(2)}, u32[]{:S(2)}) %all-to-all-start.1) | async-done | bytes 4194336 | tf_op jit(solution)/shard_map/all_to_all | solution.py:79
  282.6 4.5 %broadcast_multiply_fusion.2 = f32[128,64,128]{2,1,0:T(8,128)} fusion(f32[128,64,128]{2,1,0:T(8,128)} %all-to-all-done.1, f32[128]{0:T(128)S(1)} %reshape.203), kind=kLoop, calls=%fused_computation.26 | loop fusion | flops 1048576 | bytes 8389120 | tf_op jit(solution)/shard_map/mul | solution.py:82
  287.1 13.5 %scatter_fusion.2 = f32[8,64,128]{2,1,0:T(8,128)S(1)} fusion(f32[8,64,128]{2,1,0:T(8,128)S(1)} %slice.25, s32[128]{0:T(128)S(1)} %reshape.254, f32[128,64,128]{2,1,0:T(8,128)} %broadcast_multiply_fusion.2), kind=kCustom, calls=%fused_computation.6 | custom fusion | flops 1048576 | bytes 12583424 | tf_op jit(solution)/shard_map/scatter-add | solution.py:84
  300.7 1.1 stack.2
  301.8 4.1 all-to-all-start.2
  305.9 2.2 convolution_bitcast_fusion.1
  308.2 26.9 %all-to-all-done.2 = bf16[8,64,1024]{2,1,0:T(8,128)(2,1)S(1)} async-done(((bf16[8,64,1024]{2,1,0:T(8,128)(2,1)}), bf16[8,64,1024]{2,1,0:T(8,128)(2,1)S(1)}, u32[]{:S(2)}, u32[]{:S(2)}) %all-to-all-start.2) | async-done | bytes 1048608 | tf_op jit(solution)/shard_map/all_to_all | solution.py:94
  335.1 1.0 convolution_bitcast_fusion
  336.1 102.7 %all-reduce.3.cloned.1.call-done = (f32[16,512]{1,0:T(8,128)}, f32[16,512]{1,0:T(8,128)}, f32[64]{0:T(128)}) async-done(((f32[16,512]{1,0:T(8,128)}, f32[16,512]{1,0:T(8,128)}, f32[64]{0:T(128)}), (f32[16,512]{1,0:T(8,128)}, f32[16,512]{1,0:T(8,128)}, f32[64]{0:T(128)})) %all-reduce.3.cloned.1.call-update) | async-done | bytes 65808 | tf_op jit(solution)/shard_map/psum | solution.py:102
  438.8 1.4 copy.85
  440.2 1.4 copy.86
  441.5 1.1 copy.87
  (38 shorter events, 0.5 us)
Async XLA Ops:
  7.2 0.8 copy-start
  7.2 64.9 %reduce-scatter.2.cloned.1.call-start = ((), (), s32[]{:S(2)}) async-start(), calls=%async_computation.4 | async-start | bytes 4718592 | tf_op jit(solution)/shard_map/reduce_scatter | solution.py:34
  12.7 0.7 copy-start.4
  12.7 1.1 copy-start.7
  80.0 10.6 %copy-start.3 = (s32[1,256]{1,0:T(1,128)S(1)}, s32[1,256]{1,0:T(1,128)}, u32[]{:S(2)}) copy-start(s32[1,256]{1,0:T(1,128)} %param.18) | copy-start | bytes 3076
  82.5 35.8 %all-to-all-start = ((bf16[64,32,512]{2,0,1:T(8,128)(2,1)}), bf16[64,32,512]{2,0,1:T(8,128)(2,1)S(1)}, u32[]{:S(2)}, u32[]{:S(2)}) async-start(bf16[64,32,512]{2,0,1:T(8,128)(2,1)} %copy.47), calls=%async_computation.1 | async-start | bytes 4194304 | tf_op jit(solution)/shard_map/all_to_all | solution.py:44
  90.7 5.7 %copy-start.5 = (s32[1,256]{1,0:T(1,128)S(1)}, s32[1,256]{1,0:T(1,128)}, u32[]{:S(2)}) copy-start(s32[1,256]{1,0:T(1,128)} %param.17) | copy-start | bytes 3076
  90.7 8.0 %copy-start.1 = (f32[64,2048]{1,0:T(8,128)S(1)}, f32[64,2048]{1,0:T(8,128)}, u32[]{:S(2)}) copy-start(f32[64,2048]{1,0:T(8,128)} %reduce-scatter.2.cloned.1.call-done) | copy-start | bytes 1572868
  135.8 26.3 %copy-start.2 = (bf16[64,1024]{1,0:T(8,128)(2,1)S(1)}, bf16[64,1024]{1,0:T(8,128)(2,1)}, u32[]{:S(2)}) copy-start(bf16[64,1024]{1,0:T(8,128)(2,1)} %param.21) | copy-start | bytes 393220
  135.8 26.3 %copy-start.6 = (f32[64]{0:T(128)S(1)}, f32[64]{0:T(128)}, u32[]{:S(2)}) copy-start(f32[64]{0:T(128)} %param.14) | copy-start | bytes 772
  224.9 57.7 %all-to-all-start.1 = ((f32[128,64,128]{2,1,0:T(8,128)}), f32[128,64,128]{2,1,0:T(8,128)}, u32[]{:S(2)}, u32[]{:S(2)}) async-start(f32[128,64,128]{2,1,0:T(8,128)} %slice.26), calls=%async_computation.2 | async-start | bytes 8388608 | tf_op jit(solution)/shard_map/all_to_all | solution.py:79
  230.3 75.6 %all-gather.2.cloned.1.call-start = ((), (), s32[]{:S(2)}) async-start(), calls=%async_computation.5 | async-start | bytes 1179648 | tf_op jit(solution)/shard_map/all_gather | solution.py:92
  301.8 33.3 %all-to-all-start.2 = ((bf16[8,64,1024]{2,1,0:T(8,128)(2,1)}), bf16[8,64,1024]{2,1,0:T(8,128)(2,1)S(1)}, u32[]{:S(2)}, u32[]{:S(2)}) async-start(bf16[8,64,1024]{2,1,0:T(8,128)(2,1)} %stack.2), calls=%async_computation.3 | async-start | bytes 2097152 | tf_op jit(solution)/shard_map/all_to_all | solution.py:94
  305.9 132.9 %all-reduce.3.cloned.1.call-start = ((), (), s32[]{:S(2)}) async-start(), calls=%async_computation.6 | async-start | bytes 132096 | tf_op jit(solution)/shard_map/psum | solution.py:102
Sparse Core Ops, SparseCore 0:
  12.9 59.1 reduce-scatter.1
  233.0 33.6 all-gather.1
  336.2 102.5 all-reduce.2
